TPU v7x, 128 devices: a whole 4x4x4 slice. The times are simulated.
128 devices in a mesh: row: 8 (over z, x_hi), col: 16 (over x_lo, y, core).
Axes of the slice: x: 4 (x_hi: 2, x_lo: 2; x = x_hi * 2 + x_lo), y: 4, z: 4, core: 2. Of those that a mesh axis runs over, the one named last changes fastest.
Arguments:
- inverse_anc: float32 [8192, 8192], P('row', 'col'), may hold values from -25 to 25, as said below
- factor: float32 [8192, 4096], P('col', 'row'), may hold values from -0.0625 to 0.0625
- pattern: int32 [16, 8], replicated, may hold values 0 or 1
- d_inverse: float32 [4096, 512], P('row'), may hold values from -2 to 2, as said below
- jac_blocks: int32 [32768, 2], P(('row', 'col')), may hold values from 0 to 7, all different within a row; in each aligned block of 256 rows (0 to 255, 256 to 511, ...) at most 128 rows name the same one
- jac_values: float32 [32768, 2, 512], P(('row', 'col')), may hold values from -0.264 to 0.264
Outputs:
- diag_inverse: float32 [4096, 512], P('row')
- variance: float32 [32768], P(('row', 'col'))
Inputs may be any that keep to these rules, and one draw needn't show every extreme that they name: `inverse_anc`: exactly symmetric. `d_inverse`: each block exactly symmetric. `jac_blocks`: each row names 2 different panels; among the rows of one device no panel is named more than 128 times, a bound that some block reaches.
All inputs are finite; a program needn't handle non-finite values.
Results may differ from a plain program's by a relative error of at most 0.0003.
Values sent between devices are 32-bit elements; how exact they have to be, the bound alone decides.
No kernel may reach another device: no remote copies, remote signals or barrier semaphores. Data moves between devices by JAX's collectives and lax.ppermute only.
A program may use at most 128 MiB of HBM per device.

v0:
```python
import jax
import jax.numpy as jnp
from jax import lax
from jax.experimental import pallas as pl
from jax.experimental.pallas import tpu as pltpu
from jax.sharding import PartitionSpec as P


NZ, NH, NL, NY, NC = 4, 2, 2, 4, 2


def row_of(z, h):
    return (z % NZ) * NH + h


def col_of(l, y, j):
    return l * NY * NC + (y % NY) * NC + j


def z_shift(k):
    return [(row_of(z, h), row_of(z + k, h)) for z in range(NZ) for h in range(NH)]


H_SWAP = [(row_of(z, h), row_of(z, 1 - h)) for z in range(NZ) for h in range(NH)]
COLS = [(l, y, j) for l in range(NL) for y in range(NY) for j in range(NC)]


def y_shift(k, other_core):
    return [(col_of(l, y, j), col_of(l, y + k, j ^ other_core(l, (y + k) % NY))) for l, y, j in COLS]


L_SWAP = [(col_of(l, y, j), col_of(1 - l, y, j if l == 0 else 1 - j)) for l, y, j in COLS]
CORE_SWAP = [(col_of(l, y, j), col_of(l, y, 1 - j)) for l, y, j in COLS]


def same_core(la, ya, lb, yb):
    dy = lax.rem(yb - ya + NY, NY)
    near = jnp.where(dy == 2, jnp.where(yb >= 2, 1, 0), jnp.where(dy == 3, 0, 1))
    return jnp.where(la != lb, lb, near)


def coordinates():
    r, c = lax.axis_index("row"), lax.axis_index("col")
    return r // NH, r % NH, c // (NY * NC), (c // NC) % NY, c % NC


TN = (((0,), (0,)), ((), ()))
UPPER = [(i, j) for i in range(4) for j in range(i, 4)]


def halves(x):
    high = x.astype(jnp.bfloat16)
    return high, (x - high.astype(jnp.float32)).astype(jnp.bfloat16)


def dot3(a, b):
    ah, al = a
    bh, bl = b

    def dot(x, y):
        return lax.dot_general(x, y, TN, preferred_element_type=jnp.float32)

    return dot(ah, bh) + (dot(ah, bl) + dot(al, bh))


def pick_kernel(a, out, main, other, sems):
    p = main.shape[0]
    z, h, l, y, j = coordinates()
    r = z * NH + h
    take = jnp.where(same_core(r // NY, r % NY, l, y) == 1, j, 1 - j)
    first = pl.multiple_of(take * p, p)
    second = pl.multiple_of((1 - take) * p, p)
    one = pltpu.make_async_copy(a.at[pl.ds(first, p)], main, sems.at[0])
    two = pltpu.make_async_copy(a.at[pl.ds(second, p)], other, sems.at[1])
    one.start()
    two.start()
    one.wait()
    two.wait()
    on_diagonal = r == l * NY + y
    rows = lax.broadcasted_iota(jnp.int32, (p, p), 0)
    cols = lax.broadcasted_iota(jnp.int32, (p, p), 1)

    @pl.when(on_diagonal)
    def _():
        out[0:p] = jnp.where(rows <= cols, main[...], other[...])
        crossing = jnp.sum(jnp.where(rows == cols, other[...], 0.0), axis=0, keepdims=True)
        out[p : p + 8] = jnp.broadcast_to(crossing, (8, p))

    @pl.when(jnp.logical_not(on_diagonal))
    def _():
        out[0:p] = main[...]
        out[p : p + 8] = jnp.zeros((8, p), jnp.float32)


def pick(a):
    p = a.shape[1]
    return pl.pallas_call(
        pick_kernel,
        out_shape=jax.ShapeDtypeStruct((p + 8, p), jnp.float32),
        in_specs=[pl.BlockSpec(memory_space=pl.ANY)],
        out_specs=pl.BlockSpec(memory_space=pltpu.VMEM),
        scratch_shapes=[
            pltpu.VMEM((p, p), jnp.float32),
            pltpu.VMEM((p, p), jnp.float32),
            pltpu.SemaphoreType.DMA((2,)),
        ],
        cost_estimate=pl.CostEstimate(flops=0, bytes_accessed=12 * p * p, transcendentals=0),
        name="pick",
    )(a)


DZ = (0, 3, 1, 2, 0, 3, 1, 2)
DH = (0, 0, 0, 0, 1, 1, 1, 1)
EARLY_A = (0, 1, 2, 3, 4)
EARLY_L = (0, 1, 2, 4, 5, 6, 8)


AHEAD = 2


def add_products(early, pattern, a_in, l_in, a_buf, l_buf, acc, a_sem, l_sem, table):
    p = acc.shape[0]
    z, h, l, y, j = coordinates()
    panel, owner = z * NH + h, l * NY + y
    stored = pattern[2 * owner + j, panel]
    diagonal = jnp.int32(-1)
    count = jnp.int32(0)
    for k in range(8):
        rk = lax.rem(z + DZ[k], NZ) * NH + (h ^ DH[k])
        la, ya = rk // NY, rk % NY
        dy = lax.rem(ya - y + NY, NY)
        slot = jnp.where(la != l, 4, 0) + jnp.where(dy == 0, 0, jnp.where(dy == 3, 1, jnp.where(dy == 1, 2, 3)))
        ready = jnp.where(dy == 2, 0, 1) if k in EARLY_A else jnp.int32(0)
        active = ready == 1 if early else ready == 0
        block = 2 * rk + jnp.where(same_core(la, ya, l, y) == 1, j, 1 - j)
        table[k] = pattern[block, panel]
        table[10 + k] = slot
        diagonal = jnp.where(jnp.logical_and(rk == owner, active), k, diagonal)
        active = jnp.logical_and(active, pattern[block, panel] * stored != 0)
        table[20 + count] = k
        count = count + jnp.where(active, 1, 0)
    table[8] = pattern[2 * owner + 1 - j, panel]
    table[20 + count] = 8
    count = count + jnp.where(jnp.logical_and(diagonal >= 0, table[8] * stored != 0), 1, 0)

    def start(t):
        k = table[20 + t]
        slot = table[10 + jnp.minimum(k, 7)]
        for kk in a_in:

            @pl.when(k == kk)
            def _():
                first = 0
                for part in a_in[kk]:
                    stop = first + part.shape[0]
                    pltpu.make_async_copy(part, a_buf.at[kk, first:stop], a_sem.at[kk]).start()
                    first = stop

        for s in l_in:
            wanted = k == 8 if s == 8 else jnp.logical_and(k < 8, slot == s)

            @pl.when(wanted)
            def _():
                pltpu.make_async_copy(l_in[s], l_buf.at[k], l_sem.at[k]).start()

    for t in range(AHEAD):

        @pl.when(t < count)
        def _():
            start(t)

    acc[...] = jnp.zeros_like(acc)
    rows = lax.broadcasted_iota(jnp.int32, (p, p), 0)
    cols = lax.broadcasted_iota(jnp.int32, (p, p), 1)

    @pl.loop(0, count)
    def _(t):
        k = table[20 + t]

        @pl.when(t + AHEAD < count)
        def _():
            start(t + AHEAD)

        @pl.when(k < 8)
        def _():
            pltpu.make_async_copy(a_in[0][0], a_buf.at[k], a_sem.at[k]).wait()

        pltpu.make_async_copy(l_in[0], l_buf.at[k], l_sem.at[k]).wait()

        @pl.when(k == diagonal)
        def _():
            both = a_buf[k, 0:p]
            crossing = a_buf[k, p : p + 1]
            a_buf[8, 0:p] = jnp.where(rows > cols, both, jnp.where(rows == cols, 0.5 * crossing, 0.0))
            a_buf[k, 0:p] = jnp.where(rows < cols, both, jnp.where(rows == cols, 0.5 * both, 0.0))

        a_high, a_low = halves((a_buf[k, 0:p] * table[k].astype(jnp.float32)).T)
        l_high, l_low = halves(l_buf[k])
        acc[...] += nn(a_high, l_high) + (nn(a_high, l_low) + nn(a_low, l_high))


def grouped(slots, refs):
    groups = {}
    for k in slots:
        count = 2 if k in (3, 7) else 1
        groups[k], refs = refs[:count], refs[count:]
    return groups, refs


def flat(a_list, slots):
    return [part for k in slots for part in a_list[k]]


def early_kernel(pattern, *refs):
    a_in, refs = grouped(EARLY_A, refs)
    l_in = dict(zip(EARLY_L, refs))
    count = len(EARLY_L)
    acc, a_buf, l_buf, a_sem, l_sem, table = refs[count:]
    add_products(True, pattern, a_in, l_in, a_buf, l_buf, acc, a_sem, l_sem, table)


def late_kernel(pattern, before, *refs):
    a_in, refs = grouped(range(8), refs)
    l_in = dict(enumerate(refs[0:9]))
    out, a_buf, l_buf, acc, sums, a_sem, l_sem, more_sem, table = refs[9:]
    p = acc.shape[0]
    q = p // 4
    z, h, l, y, j = coordinates()
    own = pltpu.make_async_copy(l_in[0], l_buf.at[9], more_sem.at[0])
    sofar = pltpu.make_async_copy(before, sums, more_sem.at[1])
    own.start()
    sofar.start()
    add_products(False, pattern, a_in, l_in, a_buf, l_buf, acc, a_sem, l_sem, table)
    own.wait()
    sofar.wait()
    factor = pattern[2 * (l * NY + y) + j, z * NH + h].astype(jnp.float32)
    half = dot3(halves(l_buf[9] * factor), halves(acc[...] + sums[...]))
    acc[...] = half
    for n, (i, k) in enumerate(UPPER):
        rows_of, cols_of = slice(i * q, (i + 1) * q), slice(k * q, (k + 1) * q)
        out[pl.ds((n // 2) * q, q), pl.ds((n % 2) * q, q)] = acc[rows_of, cols_of] + acc[cols_of, rows_of].T


def buffers(p, l_count):
    return [
        pltpu.VMEM((9, p + 8, p), jnp.float32),
        pltpu.VMEM((l_count, p, p), jnp.float32),
    ]


def copies():
    return [pltpu.SemaphoreType.DMA((9,)), pltpu.SemaphoreType.DMA((9,))]


def couple_early(pattern, a_list, l_list):
    p = l_list[0].shape[0]
    anywhere = pl.BlockSpec(memory_space=pl.ANY)
    return pl.pallas_call(
        early_kernel,
        out_shape=jax.ShapeDtypeStruct((p, p), jnp.float32),
        in_specs=[pl.BlockSpec(memory_space=pltpu.SMEM)] + [anywhere] * (len(flat(a_list, EARLY_A)) + len(EARLY_L)),
        out_specs=pl.BlockSpec(memory_space=pltpu.VMEM),
        scratch_shapes=buffers(p, 9) + copies() + [pltpu.SMEM((32,), jnp.int32)],
        compiler_params=pltpu.CompilerParams(vmem_limit_bytes=28 << 20),
        cost_estimate=pl.CostEstimate(flops=30 * p**3, bytes_accessed=11 * p * p * 4, transcendentals=0),
        name="couple_early",
    )(pattern, *flat(a_list, EARLY_A), *[l_list[k] for k in EARLY_L])


def couple_late(pattern, before, a_list, l_list):
    p = l_list[0].shape[0]
    anywhere = pl.BlockSpec(memory_space=pl.ANY)
    return pl.pallas_call(
        late_kernel,
        out_shape=jax.ShapeDtypeStruct((5 * (p // 4), p // 2), jnp.float32),
        in_specs=[pl.BlockSpec(memory_space=pltpu.SMEM)] + [anywhere] * (1 + len(flat(a_list, range(8))) + len(l_list)),
        out_specs=pl.BlockSpec(memory_space=pltpu.VMEM),
        scratch_shapes=buffers(p, 10)
        + [pltpu.VMEM((p, p), jnp.float32)] * 2
        + copies()
        + [pltpu.SemaphoreType.DMA((2,)), pltpu.SMEM((32,), jnp.int32)],
        compiler_params=pltpu.CompilerParams(vmem_limit_bytes=28 << 20),
        cost_estimate=pl.CostEstimate(flops=40 * p**3, bytes_accessed=13 * p * p * 4, transcendentals=0),
        name="couple_late",
    )(pattern, before, *flat(a_list, range(8)), *l_list)


def thirds(x):
    high = x.astype(jnp.bfloat16)
    rest = x - high.astype(jnp.float32)
    middle = rest.astype(jnp.bfloat16)
    return high, middle, (rest - middle.astype(jnp.float32)).astype(jnp.bfloat16)


def indicator(mask):
    return jnp.where(mask, 1.0, 0.0)


def nn(x, y):
    return jnp.dot(x, y, preferred_element_type=jnp.float32)


def slot_kernel(panels, values, *outs):
    slotted, across, places = outs[0:4], outs[4], outs[5]
    items = panels.shape[1]
    n_panels = 8
    capacity = slotted[0].shape[0]
    slots = n_panels * capacity
    z, h = coordinates()[0:2]
    before = indicator(
        lax.broadcasted_iota(jnp.int32, (items, items), 0) < lax.broadcasted_iota(jnp.int32, (items, items), 1)
    ).astype(jnp.bfloat16)
    panel_of = lax.broadcasted_iota(jnp.int32, (n_panels, items), 0)
    slot_of = lax.broadcasted_iota(jnp.int32, (slots, items), 0)
    base = jnp.zeros((n_panels, 1), jnp.float32)
    total = None
    for k in range(2):
        panel = panels[k : k + 1, :]
        member = indicator(panel_of == panel)
        rank = nn(member.astype(jnp.bfloat16), before) + base
        base = base + jnp.sum(member, axis=1, keepdims=True)
        place = jnp.sum(member * rank, axis=0, keepdims=True).astype(jnp.int32)
        places[k : k + 1, :] = place
        away = jnp.bitwise_and(panel // NH - z + NZ, NZ - 1) + NZ * jnp.bitwise_xor(jnp.bitwise_and(panel, NH - 1), h)
        chosen = indicator(slot_of == away * capacity + place).astype(jnp.bfloat16)
        for piece in thirds(values[:, k, :]):
            part = nn(chosen, piece)
            total = part if total is None else total + part
    for k in range(NZ):
        slotted[k][...] = total[k * capacity : (k + 1) * capacity]
    across[...] = total[NZ * capacity :]


def slot_entries(panels, values, capacity):
    items, _, p = values.shape
    return pl.pallas_call(
        slot_kernel,
        out_shape=(jax.ShapeDtypeStruct((capacity, p), jnp.float32),) * NZ
        + (jax.ShapeDtypeStruct((NZ * capacity, p), jnp.float32), jax.ShapeDtypeStruct((2, items), jnp.int32)),
        in_specs=[pl.BlockSpec(memory_space=pltpu.VMEM)] * 2,
        out_specs=(pl.BlockSpec(memory_space=pltpu.VMEM),) * 6,
        cost_estimate=pl.CostEstimate(flops=12 * capacity * 8 * items * p, bytes_accessed=12 * items * p * 4, transcendentals=0),
        name="slot_entries",
    )(panels, values)


def forms_kernel(packed, d, *refs):
    xs, out, forms = refs[0:8], refs[8], refs[9]
    parts, total, x_buf, sems = refs[10:]
    p = d.shape[0]
    q = p // 4
    capacity = forms.shape[1]
    z, h = coordinates()[0:2]
    first_in = pltpu.make_async_copy(packed, parts, sems.at[0])
    second_in = pltpu.make_async_copy(d, total, sems.at[1])
    first_in.start()
    second_in.start()
    loads = []
    for k in range(8):
        load = pltpu.make_async_copy(xs[k].at[0:capacity], x_buf.at[k], sems.at[2 + k])
        load.start()
        loads.append(load)
    first_in.wait()
    second_in.wait()
    pieces = parts[...].reshape(-1, packed.shape[2])
    for n, (i, j) in enumerate(UPPER):
        rows, cols = slice(i * q, (i + 1) * q), slice(j * q, (j + 1) * q)
        block = pieces[(n // 2) * q : (n // 2 + 1) * q, (n % 2) * q : (n % 2 + 1) * q]
        total[rows, cols] += block
        if i != j:
            total[cols, rows] += block.T
    store = pltpu.make_async_copy(total, out, sems.at[10])
    store.start()
    high, low = halves(total[...])
    for first in range(2):
        for load in loads[4 * first : 4 * first + 4]:
            load.wait()
        here = x_buf[4 * first : 4 * first + 4].reshape(4 * capacity, p)
        x_high, x_low = halves(here)
        terms = (nn(x_high, high) + (nn(x_high, low) + nn(x_low, high))) * here
        lanes = terms[:, 0:q] + terms[:, q : 2 * q] + (terms[:, 2 * q : 3 * q] + terms[:, 3 * q :])
        for n in range(4):
            mine = lanes[n * capacity : (n + 1) * capacity, :]
            source = lax.rem(z - n + NZ, NZ) * NH + (h ^ first)
            forms[pl.ds(source, 1), :] = jnp.sum(mine.T, axis=0, keepdims=True)
    store.wait()


def forms_of(packed, d, xs, capacity):
    p = d.shape[0]
    return pl.pallas_call(
        forms_kernel,
        out_shape=(
            jax.ShapeDtypeStruct(d.shape, jnp.float32),
            jax.ShapeDtypeStruct((8, capacity), jnp.float32),
        ),
        in_specs=[pl.BlockSpec(memory_space=pl.ANY)] * 10,
        out_specs=(pl.BlockSpec(memory_space=pl.ANY), pl.BlockSpec(memory_space=pltpu.VMEM)),
        scratch_shapes=[
            pltpu.VMEM(packed.shape, jnp.float32),
            pltpu.VMEM((p, p), jnp.float32),
            pltpu.VMEM((8, capacity, p), jnp.float32),
            pltpu.SemaphoreType.DMA((11,)),
        ],
        compiler_params=pltpu.CompilerParams(vmem_limit_bytes=24 << 20),
        cost_estimate=pl.CostEstimate(flops=48 * capacity * p * p, bytes_accessed=20 * p * p, transcendentals=0),
        name="forms",
    )(packed, d, *xs)


def finish_kernel(panels, places, answers, out):
    n_panels, capacity = answers.shape
    items = panels.shape[1]
    panel_of = lax.broadcasted_iota(jnp.int32, (n_panels, items), 0)
    place_of = lax.broadcasted_iota(jnp.int32, (capacity, items), 0)
    pieces = thirds(answers[...])
    total = jnp.zeros((1, items), jnp.float32)
    for k in range(2):
        chosen = indicator(place_of == places[k : k + 1, :]).astype(jnp.bfloat16)
        columns = nn(pieces[0], chosen) + nn(pieces[1], chosen) + nn(pieces[2], chosen)
        member = panel_of == panels[k : k + 1, :]
        total += jnp.sum(jnp.where(member, columns, 0.0), axis=0, keepdims=True)
    out[...] = total


def finish(panels, places, answers):
    return pl.pallas_call(
        finish_kernel,
        out_shape=jax.ShapeDtypeStruct((1, panels.shape[1]), jnp.float32),
        in_specs=[pl.BlockSpec(memory_space=pltpu.VMEM)] * 3,
        out_specs=pl.BlockSpec(memory_space=pltpu.VMEM),
        name="finish",
    )(panels, places, answers)


def exchange(x, axis):
    return lax.all_to_all(x, axis, split_axis=0, concat_axis=0, tiled=True)


def body(inverse_anc, factor, pattern, d_inverse, jac_blocks, jac_values):
    p = factor.shape[0]
    n_row = lax.axis_size("row")
    n_col = lax.axis_size("col")

    panels = jac_blocks.T
    capacity = 2 * jac_values.shape[0] * jac_values.shape[1] // n_row

    def keep(lb, yb):
        return 0

    def turn(lb, yb):
        return 1

    def turn_low(lb, yb):
        return 0 if yb >= 2 else 1

    l0 = factor
    l1 = lax.ppermute(l0, "col", L_SWAP)
    l0m = lax.ppermute(l0, "col", y_shift(1, keep))
    l0p = lax.ppermute(l0, "col", y_shift(-1, turn))
    a0 = pick(inverse_anc)
    a0m = lax.ppermute(a0, "row", z_shift(1))
    a0p = lax.ppermute(a0, "row", z_shift(-1))
    l_core = lax.ppermute(l0, "col", CORE_SWAP)
    a1 = lax.ppermute(a0, "row", H_SWAP)
    l1m = lax.ppermute(l1, "col", y_shift(1, keep))
    l1p = lax.ppermute(l1, "col", y_shift(-1, keep))
    cut = (p // 16 + 1) * 8
    a0f = (lax.ppermute(a0m[:cut], "row", z_shift(1)), lax.ppermute(a0p[cut:], "row", z_shift(-1)))
    l0f = lax.ppermute(l0m, "col", y_shift(1, turn_low))
    a1m = lax.ppermute(a1, "row", z_shift(1))
    a1p = lax.ppermute(a1, "row", z_shift(-1))
    l1f = lax.ppermute(l1p, "col", y_shift(-1, keep))
    a1f = (lax.ppermute(a0f[0], "row", H_SWAP), lax.ppermute(a0f[1], "row", H_SWAP))
    a_list = [(a0,), (a0m,), (a0p,), a0f, (a1,), (a1m,), (a1p,), a1f]
    l_list = [l0, l0m, l0p, l0f, l1, l1m, l1p, l1f, l_core]
    before = couple_early(pattern, a_list, l_list)
    partial_value = couple_late(pattern, before, a_list, l_list)
    *slotted, across, places = slot_entries(panels, jac_values, capacity)
    crossed = lax.ppermute(across, "row", H_SWAP)
    xs = [slotted[0]] + [lax.ppermute(slotted[k], "row", z_shift(k)) for k in range(1, NZ)] + [crossed]
    for k in range(1, NZ):
        xs.append(lax.ppermute(crossed[k * capacity : (k + 1) * capacity], "row", z_shift(k)))
    pieces = partial_value.reshape(n_col, -1, p // 2)
    pieces = exchange(pieces, "col")
    own = jnp.sum(pieces, axis=0)
    whole = exchange(jnp.broadcast_to(own[None], pieces.shape), "col")
    diag_block, forms = forms_of(whole, d_inverse, xs, capacity)
    answers = exchange(forms, "row")
    variance = finish(panels, places, answers).reshape(-1)
    return (diag_block, variance)


def solution(mesh):
    return jax.shard_map(
        body,
        mesh=mesh,
        in_specs=(
            P("row", "col"),
            P("col", "row"),
            P(),
            P("row", None),
            P(("row", "col"), None),
            P(("row", "col"), None, None),
        ),
        out_specs=(P("row", None), P(("row", "col"))),
        check_vma=False,
    )
```

profile of v0, /device:TPU:24, one launch (start us, length us, event | category | flops | bytes accessed | tf_op | source)
XLA Modules:
  0.0 217.3 jit_solution(9409126266472415584)
XLA Ops:
  2.3 2.6 %pick.1.refs_0_ = f32[520,512]{1,0:T(8,128)} custom-call(f32[1024,512]{1,0:T(8,128)} %a.1), custom_call_target="tpu_custom_call" | custom-call | bytes 3145728 | tf_op jit(solution)/shard_map/pick/pallas_call | solution.py:97
  6.9 2.2 %collective-permute-start.1 = (f32[520,512]{1,0:T(8,128)}, f32[520,512]{1,0:T(8,128)S(1)}, u32[]{:S(2)}, u32[]{:S(2)}) collective-permute-start(f32[520,512]{1,0:T(8,128)} %pick.1.refs_0_), channel_id=1, source_target_pairs={{0,96},{16,112},{32,0},{48,16},{64,32},{80,48},{96,64},{112,80},{1... | collective-permute-start | bytes 3194888 | tf_op jit(solution)/shard_map/ppermute | solution.py:463
  9.1 2.7 %collective-permute-start.4 = (f32[520,512]{1,0:T(8,128)}, f32[520,512]{1,0:T(8,128)}, u32[]{:S(2)}, u32[]{:S(2)}) collective-permute-start(f32[520,512]{1,0:T(8,128)} %pick.1.refs_0_), channel_id=1, source_target_pairs={{0,16},{16,0},{32,48},{48,32},{64,80},{80,64},{96,112},{112,96},{1... | collective-permute-start | bytes 3194888 | tf_op jit(solution)/shard_map/ppermute | solution.py:465
  11.9 14.2 %collective-permute-done.7.refs_9_.refs_14_ = f32[512,512]{1,0:T(8,128)} collective-permute-done((f32[512,512]{1,0:T(8,128)}, f32[512,512]{1,0:T(8,128)}, u32[]{:S(2)}, u32[]{:S(2)}) %collective-permute-start.7) | collective-permute-done | bytes 1048608 | tf_op jit(solution)/shard_map/ppermute | solution.py:458
  26.4 6.7 %collective-permute-done.refs_1_ = f32[520,512]{1,0:T(8,128)S(1)} collective-permute-done((f32[520,512]{1,0:T(8,128)}, f32[520,512]{1,0:T(8,128)S(1)}, u32[]{:S(2)}, u32[]{:S(2)}) %collective-permute-start) | collective-permute-done | bytes 1064992 | tf_op jit(solution)/shard_map/ppermute | solution.py:462
  35.4 3.2 %collective-permute-done.6.refs_8_.refs_12_ = f32[512,512]{1,0:T(8,128)S(1)} collective-permute-done((f32[512,512]{1,0:T(8,128)S(1)}, f32[512,512]{1,0:T(8,128)S(1)}, u32[]{:S(2)}, u32[]{:S(2)}) %collective-permute-start.6) | collective-permute-done | bytes 1048608 | tf_op jit(solution)/shard_map/ppermute | solution.py:460
  41.2 11.0 %collective-permute-done.5.refs_7_.refs_11_ = f32[512,512]{1,0:T(8,128)} collective-permute-done((f32[512,512]{1,0:T(8,128)S(1)}, f32[512,512]{1,0:T(8,128)}, u32[]{:S(2)}, u32[]{:S(2)}) %collective-permute-start.5) | collective-permute-done | bytes 1048608 | tf_op jit(solution)/shard_map/ppermute | solution.py:459
  53.6 4.1 %collective-permute-start.12 = (f32[520,512]{1,0:T(8,128)}, f32[520,512]{1,0:T(8,128)}, u32[]{:S(2)}, u32[]{:S(2)}) collective-permute-start(f32[520,512]{1,0:T(8,128)} %collective-permute-done.4.refs_5_), channel_id=1, source_target_pairs={{0,96},{16,112},{32,0},{48,16},{64,32},{80,48},{96,64},{112,80},{1... | collective-permute-start | bytes 3194888 | tf_op jit(solution)/shard_map/ppermute | solution.py:472
  57.8 2.9 %collective-permute-done.9.refs_11_.refs_16_ = f32[512,512]{1,0:T(8,128)} collective-permute-done((f32[512,512]{1,0:T(8,128)}, f32[512,512]{1,0:T(8,128)}, u32[]{:S(2)}, u32[]{:S(2)}) %collective-permute-start.9) | collective-permute-done | bytes 1048608 | tf_op jit(solution)/shard_map/ppermute | solution.py:467
  60.7 17.8 %collective-permute-done.8.refs_10_.refs_15_ = f32[512,512]{1,0:T(8,128)S(1)} collective-permute-done((f32[512,512]{1,0:T(8,128)}, f32[512,512]{1,0:T(8,128)S(1)}, u32[]{:S(2)}, u32[]{:S(2)}) %collective-permute-start.8) | collective-permute-done | bytes 1048608 | tf_op jit(solution)/shard_map/ppermute | solution.py:466
  79.5 2.5 %collective-permute-start.13 = (f32[264,512]{1,0:T(8,128)}, f32[264,512]{1,0:T(8,128)}, u32[]{:S(2)}, u32[]{:S(2)}) collective-permute-start(f32[264,512]{1,0:T(8,128)} %collective-permute-done.2.refs_3_), channel_id=1, source_target_pairs={{0,16},{16,0},{32,48},{48,32},{64,80},{80,64},{96,112},{112,96},{1... | collective-permute-start | bytes 1622024 | tf_op jit(solution)/shard_map/ppermute | solution.py:474
  82.1 18.0 %collective-permute-done.15.refs_13_ = f32[512,512]{1,0:T(8,128)S(1)} collective-permute-done((f32[512,512]{1,0:T(8,128)}, f32[512,512]{1,0:T(8,128)S(1)}, u32[]{:S(2)}, u32[]{:S(2)}) %collective-permute-start.15) | collective-permute-done | bytes 1048608 | tf_op jit(solution)/shard_map/ppermute | solution.py:470
  101.1 2.8 %collective-permute-start.14 = (f32[256,512]{1,0:T(8,128)}, f32[256,512]{1,0:T(8,128)}, u32[]{:S(2)}, u32[]{:S(2)}) collective-permute-start(f32[256,512]{1,0:T(8,128)} %copy-done.17), channel_id=1, source_target_pairs={{0,16},{16,0},{32,48},{48,32},{64,80},{80,64},{96,112},{112,96},{1... | collective-permute-start | bytes 1572872 | tf_op jit(solution)/shard_map/ppermute | solution.py:474
  104.0 9.1 %slot_entries.1 = (f32[128,512]{1,0:T(8,128)}, f32[128,512]{1,0:T(8,128)}, f32[128,512]{1,0:T(8,128)}, f32[128,512]{1,0:T(8,128)}, f32[512,512]{1,0:T(8,128)}, /*index=5*/s32[2,256]{1,0:T(2,128)}) custom-call(s32[2,256]{1,0:T(2,128)} %bitcast.10, f32[256,2,512]{2,1,0:T(2,128)} %values.1), custom_call_target="tpu_custom_call" | custom-call | flops 1610612736 | bytes 6291456 | tf_op jit(solution)/shard_map/slot_entries/pallas_call | solution.py:336
  120.2 3.8 %collective-permute-start.20 = (f32[512,512]{1,0:T(8,128)}, f32[512,512]{1,0:T(8,128)S(1)}, u32[]{:S(2)}, u32[]{:S(2)}) collective-permute-start(f32[512,512]{1,0:T(8,128)} %get-tuple-element.14), channel_id=1, source_target_pairs={{0,16},{16,0},{32,48},{48,32},{64,80},{80,64},{96,112},{112,96},{1... | collective-permute-start | bytes 3145736 | tf_op jit(solution)/shard_map/ppermute | solution.py:480
  124.1 2.5 %couple_late.1 = f32[640,256]{1,0:T(8,128)S(1)} custom-call(s32[16,8]{1,0:T(8,128)S(1)} %copy.11.pattern, f32[512,512]{1,0:T(8,128)S(1)} %couple_early.1.before, f32[520,512]{1,0:T(8,128)S(1)} %copy-done, f32[520,512]{1,0:T(8,128)S(1)} %collective-permute-done.refs_1_, f32[520,512]{1,0:T(8,128)S(1)} %copy-done.3, f32[264,512]{1,0:T(8,128)} %collective-permute-done.2.refs_3_, ...), custom_call_target="tpu_custom_call" | custom-call | flops 5368709120 | bytes 13631488 | tf_op jit(solution)/shard_map/couple_late/pallas_call | solution.py:273
  126.6 26.3 %all_to_all.21 = f32[16,40,256]{2,1,0:T(8,128)S(1)} all-to-all(f32[16,40,256]{2,1,0:T(8,128)S(1)} %bitcast.7), channel_id=1, replica_groups=mesh['row'=8,'col'=16] {'col'}, dimensions={0} | all-to-all | bytes 1310720 | tf_op jit(solution)/shard_map/all_to_all | solution.py:437
  153.8 11.0 %all-to-all-start.1 = ((f32[16,40,256]{2,1,0:T(8,128)}), f32[16,40,256]{2,1,0:T(8,128)S(1)}, u32[]{:S(2)}, u32[]{:S(2)}) async-start(f32[16,40,256]{2,1,0:T(8,128)} %broadcast_in_dim.2), calls=%async_computation.1 | async-start | bytes 1310720 | tf_op jit(solution)/shard_map/all_to_all | solution.py:437
  164.9 3.6 %collective-permute-start.18 = (f32[128,512]{1,0:T(8,128)}, f32[128,512]{1,0:T(8,128)S(1)}, u32[]{:S(2)}, u32[]{:S(2)}) collective-permute-start(f32[128,512]{1,0:T(8,128)} %get-tuple-element.12), channel_id=1, source_target_pairs={{0,64},{16,80},{32,96},{48,112},{64,0},{80,16},{96,32},{112,48},{1... | collective-permute-start | bytes 786440 | tf_op jit(solution)/shard_map/ppermute | solution.py:481
  168.5 2.5 %collective-permute-start.19 = (f32[128,512]{1,0:T(8,128)S(1)}, f32[128,512]{1,0:T(8,128)S(1)}, u32[]{:S(2)}, u32[]{:S(2)}) collective-permute-start(f32[128,512]{1,0:T(8,128)S(1)} %copy-done.32), channel_id=1, source_target_pairs={{0,96},{16,112},{32,0},{48,16},{64,32},{80,48},{96,64},{112,80},{1... | collective-permute-start | bytes 786440 | tf_op jit(solution)/shard_map/ppermute | solution.py:481
  174.6 11.2 %collective-permute-start.21 = (f32[128,512]{1,0:T(8,128)S(1)}, f32[128,512]{1,0:T(8,128)S(1)}, u32[]{:S(2)}, u32[]{:S(2)}) collective-permute-start(f32[128,512]{1,0:T(8,128)S(1)} %get-tuple-element.20), channel_id=1, source_target_pairs={{0,32},{16,48},{32,64},{48,80},{64,96},{80,112},{96,0},{112,16},{1... | collective-permute-start | bytes 786440 | tf_op jit(solution)/shard_map/ppermute | solution.py:483
  189.0 3.0 %collective-permute-done.21.refs_5_ = f32[128,512]{1,0:T(8,128)S(1)} collective-permute-done((f32[128,512]{1,0:T(8,128)S(1)}, f32[128,512]{1,0:T(8,128)S(1)}, u32[]{:S(2)}, u32[]{:S(2)}) %collective-permute-start.21) | collective-permute-done | bytes 262176 | tf_op jit(solution)/shard_map/ppermute | solution.py:483
  198.5 2.9 %forms.1 = (f32[512,512]{1,0:T(8,128)}, f32[8,128]{1,0:T(8,128)S(1)}) custom-call(f32[16,40,256]{2,1,0:T(8,128)S(1)} %all-to-all-done.1.packed, f32[512,512]{1,0:T(8,128)S(1)} %copy-done.6, f32[128,512]{1,0:T(8,128)S(1)} %copy-done.30, f32[128,512]{1,0:T(8,128)S(1)} %collective-permute-done.17.refs_1_, f32[128,512]{1,0:T(8,128)S(1)} %copy-done.21, ...), custom_call_target="tpu_custom_call" | custom-call | flops 1610612736 | bytes 5242880 | tf_op jit(solution)/shard_map/forms/pallas_call | solution.py:391
  201.4 14.5 %all_to_all.22 = f32[8,1,128]{2,1,0:T(1,128)} all-to-all(f32[8,1,128]{2,1,0:T(1,128)S(1)} %bitcast.8), channel_id=1, replica_groups=mesh['row'=8,'col'=16] {'row'}, dimensions={0} | all-to-all | bytes 8192 | tf_op jit(solution)/shard_map/all_to_all | solution.py:437
  (106 shorter events, 35.1 us)
Async XLA Ops:
  0.6 11.2 %collective-permute-start.10 = (f32[512,512]{1,0:T(8,128)}, f32[512,512]{1,0:T(8,128)S(1)}, u32[]{:S(2)}, u32[]{:S(2)}) collective-permute-start(f32[512,512]{1,0:T(8,128)} %refs_10_.1), channel_id=1, source_target_pairs={{0,1},{1,0},{2,3},{3,2},{4,5},{5,4},{6,7},{7,6},{8,9},{9,8},{10,11... | collective-permute-start | bytes 3145736 | tf_op jit(solution)/shard_map/ppermute | solution.py:464
  0.7 25.4 %collective-permute-start.7 = (f32[512,512]{1,0:T(8,128)}, f32[512,512]{1,0:T(8,128)}, u32[]{:S(2)}, u32[]{:S(2)}) collective-permute-start(f32[512,512]{1,0:T(8,128)} %refs_10_.1), channel_id=1, source_target_pairs={{0,8},{1,9},{2,10},{3,11},{4,12},{5,13},{6,14},{7,15},{8,1},{9,0},... | collective-permute-start | bytes 3145736 | tf_op jit(solution)/shard_map/ppermute | solution.py:458
  4.9 28.1 %collective-permute-start = (f32[520,512]{1,0:T(8,128)}, f32[520,512]{1,0:T(8,128)S(1)}, u32[]{:S(2)}, u32[]{:S(2)}) collective-permute-start(f32[520,512]{1,0:T(8,128)} %pick.1.refs_0_), channel_id=1, source_target_pairs={{0,32},{16,48},{32,64},{48,80},{64,96},{80,112},{96,0},{112,16},{1... | collective-permute-start | bytes 3194888 | tf_op jit(solution)/shard_map/ppermute | solution.py:462
  6.9 26.9 %collective-permute-start.1 = (f32[520,512]{1,0:T(8,128)}, f32[520,512]{1,0:T(8,128)S(1)}, u32[]{:S(2)}, u32[]{:S(2)}) collective-permute-start(f32[520,512]{1,0:T(8,128)} %pick.1.refs_0_), channel_id=1, source_target_pairs={{0,96},{16,112},{32,0},{48,16},{64,32},{80,48},{96,64},{112,80},{1... | collective-permute-start | bytes 3194888 | tf_op jit(solution)/shard_map/ppermute | solution.py:463
  9.1 44.5 %collective-permute-start.4 = (f32[520,512]{1,0:T(8,128)}, f32[520,512]{1,0:T(8,128)}, u32[]{:S(2)}, u32[]{:S(2)}) collective-permute-start(f32[520,512]{1,0:T(8,128)} %pick.1.refs_0_), channel_id=1, source_target_pairs={{0,16},{16,0},{32,48},{48,32},{64,80},{80,64},{96,112},{112,96},{1... | collective-permute-start | bytes 3194888 | tf_op jit(solution)/shard_map/ppermute | solution.py:465
  11.9 26.7 %collective-permute-start.6 = (f32[512,512]{1,0:T(8,128)S(1)}, f32[512,512]{1,0:T(8,128)S(1)}, u32[]{:S(2)}, u32[]{:S(2)}) collective-permute-start(f32[512,512]{1,0:T(8,128)S(1)} %copy-done.4), channel_id=1, source_target_pairs={{0,7},{1,6},{2,1},{3,0},{4,3},{5,2},{6,5},{7,4},{8,15},{9,14},{10,... | collective-permute-start | bytes 3145736 | tf_op jit(solution)/shard_map/ppermute | solution.py:460
  26.2 26.1 %collective-permute-start.5 = (f32[512,512]{1,0:T(8,128)S(1)}, f32[512,512]{1,0:T(8,128)}, u32[]{:S(2)}, u32[]{:S(2)}) collective-permute-start(f32[512,512]{1,0:T(8,128)S(1)} %copy-done.4), channel_id=1, source_target_pairs={{0,2},{1,3},{2,4},{3,5},{4,6},{5,7},{6,0},{7,1},{8,10},{9,11},{10,... | collective-permute-start | bytes 3145736 | tf_op jit(solution)/shard_map/ppermute | solution.py:459
  33.1 27.6 %collective-permute-start.9 = (f32[512,512]{1,0:T(8,128)}, f32[512,512]{1,0:T(8,128)}, u32[]{:S(2)}, u32[]{:S(2)}) collective-permute-start(f32[512,512]{1,0:T(8,128)} %collective-permute-done.7.refs_9_.refs_14_), channel_id=1, source_target_pairs={{0,6},{1,7},{2,0},{3,1},{4,2},{5,3},{6,4},{7,5},{8,14},{9,15},{10,... | collective-permute-start | bytes 3145736 | tf_op jit(solution)/shard_map/ppermute | solution.py:467
  33.9 23.9 %collective-permute-start.2 = (f32[264,512]{1,0:T(8,128)S(1)}, f32[264,512]{1,0:T(8,128)}, u32[]{:S(2)}, u32[]{:S(2)}) collective-permute-start(f32[264,512]{1,0:T(8,128)S(1)} %slice.20), channel_id=1, source_target_pairs={{0,32},{16,48},{32,64},{48,80},{64,96},{80,112},{96,0},{112,16},{1... | collective-permute-start | bytes 1622024 | tf_op jit(solution)/shard_map/ppermute | solution.py:469
  39.6 14.1 %collective-permute-start.3 = (f32[256,512]{1,0:T(8,128)S(1)}, f32[256,512]{1,0:T(8,128)S(1)}, u32[]{:S(2)}, u32[]{:S(2)}) collective-permute-start(f32[256,512]{1,0:T(8,128)S(1)} %slice.21), channel_id=1, source_target_pairs={{0,96},{16,112},{32,0},{48,16},{64,32},{80,48},{96,64},{112,80},{1... | collective-permute-start | bytes 1572872 | tf_op jit(solution)/shard_map/ppermute | solution.py:469
  52.2 26.2 %collective-permute-start.8 = (f32[512,512]{1,0:T(8,128)}, f32[512,512]{1,0:T(8,128)S(1)}, u32[]{:S(2)}, u32[]{:S(2)}) collective-permute-start(f32[512,512]{1,0:T(8,128)} %collective-permute-done.7.refs_9_.refs_14_), channel_id=1, source_target_pairs={{0,2},{1,3},{2,4},{3,5},{4,6},{5,7},{6,0},{7,1},{8,10},{9,11},{10,... | collective-permute-start | bytes 3145736 | tf_op jit(solution)/shard_map/ppermute | solution.py:466
  53.6 46.6 %collective-permute-start.15 = (f32[512,512]{1,0:T(8,128)}, f32[512,512]{1,0:T(8,128)S(1)}, u32[]{:S(2)}, u32[]{:S(2)}) collective-permute-start(f32[512,512]{1,0:T(8,128)} %collective-permute-done.5.refs_7_.refs_11_), channel_id=1, source_target_pairs={{0,3},{1,2},{2,4},{3,5},{4,6},{5,7},{6,1},{7,0},{8,11},{9,10},{10,... | collective-permute-start | bytes 3145736 | tf_op jit(solution)/shard_map/ppermute | solution.py:470
  53.6 70.4 %collective-permute-start.12 = (f32[520,512]{1,0:T(8,128)}, f32[520,512]{1,0:T(8,128)}, u32[]{:S(2)}, u32[]{:S(2)}) collective-permute-start(f32[520,512]{1,0:T(8,128)} %collective-permute-done.4.refs_5_), channel_id=1, source_target_pairs={{0,96},{16,112},{32,0},{48,16},{64,32},{80,48},{96,64},{112,80},{1... | collective-permute-start | bytes 3194888 | tf_op jit(solution)/shard_map/ppermute | solution.py:472
  57.7 66.3 %collective-permute-start.11 = (f32[520,512]{1,0:T(8,128)}, f32[520,512]{1,0:T(8,128)}, u32[]{:S(2)}, u32[]{:S(2)}) collective-permute-start(f32[520,512]{1,0:T(8,128)} %collective-permute-done.4.refs_5_), channel_id=1, source_target_pairs={{0,32},{16,48},{32,64},{48,80},{64,96},{80,112},{96,0},{112,16},{1... | collective-permute-start | bytes 3194888 | tf_op jit(solution)/shard_map/ppermute | solution.py:471
  60.7 63.3 %collective-permute-start.16 = (f32[512,512]{1,0:T(8,128)}, f32[512,512]{1,0:T(8,128)}, u32[]{:S(2)}, u32[]{:S(2)}) collective-permute-start(f32[512,512]{1,0:T(8,128)} %collective-permute-done.9.refs_11_.refs_16_), channel_id=1, source_target_pairs={{0,6},{1,7},{2,0},{3,1},{4,2},{5,3},{6,4},{7,5},{8,14},{9,15},{10,... | collective-permute-start | bytes 3145736 | tf_op jit(solution)/shard_map/ppermute | solution.py:473
  79.5 44.5 %collective-permute-start.13 = (f32[264,512]{1,0:T(8,128)}, f32[264,512]{1,0:T(8,128)}, u32[]{:S(2)}, u32[]{:S(2)}) collective-permute-start(f32[264,512]{1,0:T(8,128)} %collective-permute-done.2.refs_3_), channel_id=1, source_target_pairs={{0,16},{16,0},{32,48},{48,32},{64,80},{80,64},{96,112},{112,96},{1... | collective-permute-start | bytes 1622024 | tf_op jit(solution)/shard_map/ppermute | solution.py:474
  101.1 19.1 %collective-permute-start.14 = (f32[256,512]{1,0:T(8,128)}, f32[256,512]{1,0:T(8,128)}, u32[]{:S(2)}, u32[]{:S(2)}) collective-permute-start(f32[256,512]{1,0:T(8,128)} %copy-done.17), channel_id=1, source_target_pairs={{0,16},{16,0},{32,48},{48,32},{64,80},{80,64},{96,112},{112,96},{1... | collective-permute-start | bytes 1572872 | tf_op jit(solution)/shard_map/ppermute | solution.py:474
  120.2 50.8 %collective-permute-start.20 = (f32[512,512]{1,0:T(8,128)}, f32[512,512]{1,0:T(8,128)S(1)}, u32[]{:S(2)}, u32[]{:S(2)}) collective-permute-start(f32[512,512]{1,0:T(8,128)} %get-tuple-element.14), channel_id=1, source_target_pairs={{0,16},{16,0},{32,48},{48,32},{64,80},{80,64},{96,112},{112,96},{1... | collective-permute-start | bytes 3145736 | tf_op jit(solution)/shard_map/ppermute | solution.py:480
  153.8 38.9 %all-to-all-start.1 = ((f32[16,40,256]{2,1,0:T(8,128)}), f32[16,40,256]{2,1,0:T(8,128)S(1)}, u32[]{:S(2)}, u32[]{:S(2)}) async-start(f32[16,40,256]{2,1,0:T(8,128)} %broadcast_in_dim.2), calls=%async_computation.1 | async-start | bytes 1310720 | tf_op jit(solution)/shard_map/all_to_all | solution.py:437
  164.9 20.9 %collective-permute-start.18 = (f32[128,512]{1,0:T(8,128)}, f32[128,512]{1,0:T(8,128)S(1)}, u32[]{:S(2)}, u32[]{:S(2)}) collective-permute-start(f32[128,512]{1,0:T(8,128)} %get-tuple-element.12), channel_id=1, source_target_pairs={{0,64},{16,80},{32,96},{48,112},{64,0},{80,16},{96,32},{112,48},{1... | collective-permute-start | bytes 786440 | tf_op jit(solution)/shard_map/ppermute | solution.py:481
  168.5 18.0 %collective-permute-start.19 = (f32[128,512]{1,0:T(8,128)S(1)}, f32[128,512]{1,0:T(8,128)S(1)}, u32[]{:S(2)}, u32[]{:S(2)}) collective-permute-start(f32[128,512]{1,0:T(8,128)S(1)} %copy-done.32), channel_id=1, source_target_pairs={{0,96},{16,112},{32,0},{48,16},{64,32},{80,48},{96,64},{112,80},{1... | collective-permute-start | bytes 786440 | tf_op jit(solution)/shard_map/ppermute | solution.py:481
  171.1 16.5 %collective-permute-start.23 = (f32[128,512]{1,0:T(8,128)S(1)}, f32[128,512]{1,0:T(8,128)S(1)}, u32[]{:S(2)}, u32[]{:S(2)}) collective-permute-start(f32[128,512]{1,0:T(8,128)S(1)} %get-tuple-element.18), channel_id=1, source_target_pairs={{0,96},{16,112},{32,0},{48,16},{64,32},{80,48},{96,64},{112,80},{1... | collective-permute-start | bytes 786440 | tf_op jit(solution)/shard_map/ppermute | solution.py:483
  171.2 17.1 %collective-permute-start.22 = (f32[128,512]{1,0:T(8,128)S(1)}, f32[128,512]{1,0:T(8,128)S(1)}, u32[]{:S(2)}, u32[]{:S(2)}) collective-permute-start(f32[128,512]{1,0:T(8,128)S(1)} %get-tuple-element.19), channel_id=1, source_target_pairs={{0,64},{16,80},{32,96},{48,112},{64,0},{80,16},{96,32},{112,48},{1... | collective-permute-start | bytes 786440 | tf_op jit(solution)/shard_map/ppermute | solution.py:483
  174.6 17.4 %collective-permute-start.21 = (f32[128,512]{1,0:T(8,128)S(1)}, f32[128,512]{1,0:T(8,128)S(1)}, u32[]{:S(2)}, u32[]{:S(2)}) collective-permute-start(f32[128,512]{1,0:T(8,128)S(1)} %get-tuple-element.20), channel_id=1, source_target_pairs={{0,32},{16,48},{32,64},{48,80},{64,96},{80,112},{96,0},{112,16},{1... | collective-permute-start | bytes 786440 | tf_op jit(solution)/shard_map/ppermute | solution.py:483
  (34 other events, 247.3 us)
where the time goes:
time: 219 us; the launch traced here: 217 us
  waiting for transfers between devices  79.3 us (36%)
  starting transfers between devices  56.3 us (26%)
  blocking collectives  40.8 us (19%)
  local copies, waits for them, and re-layouts  20.3 us (9%)
  Pallas kernels  19.7 us (9%)
    all_to_all x2, blocking collectives, exchange(): return lax.all_to_all(x, axis, split_axis=0, concat_axis=0, tiled=True)  40.8 us
    unnamed x67, local copies, waits for them, and re-layouts  19.3 us
    ppermute x1, waiting for transfers between devices, body(): l0f = lax.ppermute(l0m, 'col', y_shift(1, turn_low))  18 us
    ppermute x1, waiting for transfers between devices, body(): l1m = lax.ppermute(l1, 'col', y_shift(1, keep))  17.8 us
    ppermute x1, waiting for transfers between devices, body(): l1 = lax.ppermute(l0, 'col', L_SWAP)  14.2 us
    ppermute x3, starting transfers between devices, body(): lax.ppermute(crossed[k * capacity:(k + 1) * capacity], 'row', z_shift(k))  12.8 us
    ppermute x1, waiting for transfers between devices, body(): l0m = lax.ppermute(l0, 'col', y_shift(1, keep))  11 us
    all_to_all x1, starting transfers between devices, exchange(): return lax.all_to_all(x, axis, split_axis=0, concat_axis=0, tiled=True)  11 us
  transfers between devices with their start and end apart: 25, of which 10 were waited for; matrix products, arithmetic and copies ran while one was open for 1% of the time, Pallas kernels for 7%

commit v1 on v0

--- a/solution.py
+++ b/solution.py
@@ -82,13 +82,13 @@
 
     @pl.when(on_diagonal)
     def _():
-        out[0:p] = jnp.where(rows <= cols, main[...], other[...])
+        out[0:p] = jnp.where(rows <= cols, main[...], other[...]).T
         crossing = jnp.sum(jnp.where(rows == cols, other[...], 0.0), axis=0, keepdims=True)
         out[p : p + 8] = jnp.broadcast_to(crossing, (8, p))
 
     @pl.when(jnp.logical_not(on_diagonal))
     def _():
-        out[0:p] = main[...]
+        out[0:p] = main[...].T
         out[p : p + 8] = jnp.zeros((8, p), jnp.float32)
 
 
@@ -115,7 +115,7 @@
 EARLY_L = (0, 1, 2, 4, 5, 6, 8)
 
 
-AHEAD = 2
+AHEAD = 4
 
 
 def add_products(early, pattern, a_in, l_in, a_buf, l_buf, acc, a_sem, l_sem, table):
@@ -191,10 +191,10 @@
         def _():
             both = a_buf[k, 0:p]
             crossing = a_buf[k, p : p + 1]
-            a_buf[8, 0:p] = jnp.where(rows > cols, both, jnp.where(rows == cols, 0.5 * crossing, 0.0))
-            a_buf[k, 0:p] = jnp.where(rows < cols, both, jnp.where(rows == cols, 0.5 * both, 0.0))
-
-        a_high, a_low = halves((a_buf[k, 0:p] * table[k].astype(jnp.float32)).T)
+            a_buf[8, 0:p] = jnp.where(rows < cols, both, jnp.where(rows == cols, 0.5 * crossing, 0.0))
+            a_buf[k, 0:p] = jnp.where(rows > cols, both, jnp.where(rows == cols, 0.5 * both, 0.0))
+
+        a_high, a_low = halves(a_buf[k, 0:p])
         l_high, l_low = halves(l_buf[k])
         acc[...] += nn(a_high, l_high) + (nn(a_high, l_low) + nn(a_low, l_high))
 

time: 219 us -> 218 us (level)
  no operation moved by 1% of the time
where the time goes in v1:
time: 218 us; the launch traced here: 217 us
  waiting for transfers between devices  79.3 us (36%)
  starting transfers between devices  55.7 us (26%)
  blocking collectives  40.8 us (19%)
  local copies, waits for them, and re-layouts  20.3 us (9%)
  Pallas kernels  20.2 us (9%)
    all_to_all x2, blocking collectives, exchange(): return lax.all_to_all(x, axis, split_axis=0, concat_axis=0, tiled=True)  40.8 us
    unnamed x67, local copies, waits for them, and re-layouts  19.3 us
    ppermute x1, waiting for transfers between devices, body(): l0f = lax.ppermute(l0m, 'col', y_shift(1, turn_low))  18 us
    ppermute x1, waiting for transfers between devices, body(): l1m = lax.ppermute(l1, 'col', y_shift(1, keep))  17.5 us
    ppermute x1, waiting for transfers between devices, body(): l1 = lax.ppermute(l0, 'col', L_SWAP)  14 us
    ppermute x3, starting transfers between devices, body(): lax.ppermute(crossed[k * capacity:(k + 1) * capacity], 'row', z_shift(k))  12.5 us
    all_to_all x1, starting transfers between devices, exchange(): return lax.all_to_all(x, axis, split_axis=0, concat_axis=0, tiled=True)  10.8 us
    ppermute x1, waiting for transfers between devices, body(): l0m = lax.ppermute(l0, 'col', y_shift(1, keep))  10.8 us
  transfers between devices with their start and end apart: 25, of which 10 were waited for; matrix products, arithmetic and copies ran while one was open for 1% of the time, Pallas kernels for 7%

profile of v1, /device:TPU:24, one launch (start us, length us, event | category | flops | bytes accessed | tf_op | source)
XLA Modules:
  0.0 217.2 jit_solution(101654955873869200)
XLA Ops:
  2.3 2.9 %pick.1.refs_0_ = f32[520,512]{1,0:T(8,128)} custom-call(f32[1024,512]{1,0:T(8,128)} %a.1), custom_call_target="tpu_custom_call" | custom-call | bytes 3145728 | tf_op jit(solution)/shard_map/pick/pallas_call | solution.py:97
  7.2 2.2 %collective-permute-start.1 = (f32[520,512]{1,0:T(8,128)}, f32[520,512]{1,0:T(8,128)S(1)}, u32[]{:S(2)}, u32[]{:S(2)}) collective-permute-start(f32[520,512]{1,0:T(8,128)} %pick.1.refs_0_), channel_id=1, source_target_pairs={{0,96},{16,112},{32,0},{48,16},{64,32},{80,48},{96,64},{112,80},{1... | collective-permute-start | bytes 3194888 | tf_op jit(solution)/shard_map/ppermute | solution.py:463
  9.4 2.7 %collective-permute-start.4 = (f32[520,512]{1,0:T(8,128)}, f32[520,512]{1,0:T(8,128)}, u32[]{:S(2)}, u32[]{:S(2)}) collective-permute-start(f32[520,512]{1,0:T(8,128)} %pick.1.refs_0_), channel_id=1, source_target_pairs={{0,16},{16,0},{32,48},{48,32},{64,80},{80,64},{96,112},{112,96},{1... | collective-permute-start | bytes 3194888 | tf_op jit(solution)/shard_map/ppermute | solution.py:465
  12.2 14.0 %collective-permute-done.7.refs_9_.refs_14_ = f32[512,512]{1,0:T(8,128)} collective-permute-done((f32[512,512]{1,0:T(8,128)}, f32[512,512]{1,0:T(8,128)}, u32[]{:S(2)}, u32[]{:S(2)}) %collective-permute-start.7) | collective-permute-done | bytes 1048608 | tf_op jit(solution)/shard_map/ppermute | solution.py:458
  26.4 6.9 %collective-permute-done.refs_1_ = f32[520,512]{1,0:T(8,128)S(1)} collective-permute-done((f32[520,512]{1,0:T(8,128)}, f32[520,512]{1,0:T(8,128)S(1)}, u32[]{:S(2)}, u32[]{:S(2)}) %collective-permute-start) | collective-permute-done | bytes 1064992 | tf_op jit(solution)/shard_map/ppermute | solution.py:462
  35.7 3.2 %collective-permute-done.6.refs_8_.refs_12_ = f32[512,512]{1,0:T(8,128)S(1)} collective-permute-done((f32[512,512]{1,0:T(8,128)S(1)}, f32[512,512]{1,0:T(8,128)S(1)}, u32[]{:S(2)}, u32[]{:S(2)}) %collective-permute-start.6) | collective-permute-done | bytes 1048608 | tf_op jit(solution)/shard_map/ppermute | solution.py:460
  41.5 10.8 %collective-permute-done.5.refs_7_.refs_11_ = f32[512,512]{1,0:T(8,128)} collective-permute-done((f32[512,512]{1,0:T(8,128)S(1)}, f32[512,512]{1,0:T(8,128)}, u32[]{:S(2)}, u32[]{:S(2)}) %collective-permute-start.5) | collective-permute-done | bytes 1048608 | tf_op jit(solution)/shard_map/ppermute | solution.py:459
  53.6 4.1 %collective-permute-start.12 = (f32[520,512]{1,0:T(8,128)}, f32[520,512]{1,0:T(8,128)}, u32[]{:S(2)}, u32[]{:S(2)}) collective-permute-start(f32[520,512]{1,0:T(8,128)} %collective-permute-done.4.refs_5_), channel_id=1, source_target_pairs={{0,96},{16,112},{32,0},{48,16},{64,32},{80,48},{96,64},{112,80},{1... | collective-permute-start | bytes 3194888 | tf_op jit(solution)/shard_map/ppermute | solution.py:472
  57.8 3.2 %collective-permute-done.9.refs_11_.refs_16_ = f32[512,512]{1,0:T(8,128)} collective-permute-done((f32[512,512]{1,0:T(8,128)}, f32[512,512]{1,0:T(8,128)}, u32[]{:S(2)}, u32[]{:S(2)}) %collective-permute-start.9) | collective-permute-done | bytes 1048608 | tf_op jit(solution)/shard_map/ppermute | solution.py:467
  61.0 17.5 %collective-permute-done.8.refs_10_.refs_15_ = f32[512,512]{1,0:T(8,128)S(1)} collective-permute-done((f32[512,512]{1,0:T(8,128)}, f32[512,512]{1,0:T(8,128)S(1)}, u32[]{:S(2)}, u32[]{:S(2)}) %collective-permute-start.8) | collective-permute-done | bytes 1048608 | tf_op jit(solution)/shard_map/ppermute | solution.py:466
  79.5 2.5 %collective-permute-start.13 = (f32[264,512]{1,0:T(8,128)}, f32[264,512]{1,0:T(8,128)}, u32[]{:S(2)}, u32[]{:S(2)}) collective-permute-start(f32[264,512]{1,0:T(8,128)} %collective-permute-done.2.refs_3_), channel_id=1, source_target_pairs={{0,16},{16,0},{32,48},{48,32},{64,80},{80,64},{96,112},{112,96},{1... | collective-permute-start | bytes 1622024 | tf_op jit(solution)/shard_map/ppermute | solution.py:474
  82.1 18.0 %collective-permute-done.15.refs_13_ = f32[512,512]{1,0:T(8,128)S(1)} collective-permute-done((f32[512,512]{1,0:T(8,128)}, f32[512,512]{1,0:T(8,128)S(1)}, u32[]{:S(2)}, u32[]{:S(2)}) %collective-permute-start.15) | collective-permute-done | bytes 1048608 | tf_op jit(solution)/shard_map/ppermute | solution.py:470
  101.1 2.8 %collective-permute-start.14 = (f32[256,512]{1,0:T(8,128)}, f32[256,512]{1,0:T(8,128)}, u32[]{:S(2)}, u32[]{:S(2)}) collective-permute-start(f32[256,512]{1,0:T(8,128)} %copy-done.17), channel_id=1, source_target_pairs={{0,16},{16,0},{32,48},{48,32},{64,80},{80,64},{96,112},{112,96},{1... | collective-permute-start | bytes 1572872 | tf_op jit(solution)/shard_map/ppermute | solution.py:474
  104.0 9.1 %slot_entries.1 = (f32[128,512]{1,0:T(8,128)}, f32[128,512]{1,0:T(8,128)}, f32[128,512]{1,0:T(8,128)}, f32[128,512]{1,0:T(8,128)}, f32[512,512]{1,0:T(8,128)}, /*index=5*/s32[2,256]{1,0:T(2,128)}) custom-call(s32[2,256]{1,0:T(2,128)} %bitcast.10, f32[256,2,512]{2,1,0:T(2,128)} %values.1), custom_call_target="tpu_custom_call" | custom-call | flops 1610612736 | bytes 6291456 | tf_op jit(solution)/shard_map/slot_entries/pallas_call | solution.py:336
  120.2 3.7 %collective-permute-start.20 = (f32[512,512]{1,0:T(8,128)}, f32[512,512]{1,0:T(8,128)S(1)}, u32[]{:S(2)}, u32[]{:S(2)}) collective-permute-start(f32[512,512]{1,0:T(8,128)} %get-tuple-element.14), channel_id=1, source_target_pairs={{0,16},{16,0},{32,48},{48,32},{64,80},{80,64},{96,112},{112,96},{1... | collective-permute-start | bytes 3145736 | tf_op jit(solution)/shard_map/ppermute | solution.py:480
  124.0 2.7 %couple_late.1 = f32[640,256]{1,0:T(8,128)S(1)} custom-call(s32[16,8]{1,0:T(8,128)S(1)} %copy.11.pattern, f32[512,512]{1,0:T(8,128)S(1)} %couple_early.1.before, f32[520,512]{1,0:T(8,128)S(1)} %copy-done, f32[520,512]{1,0:T(8,128)S(1)} %collective-permute-done.refs_1_, f32[520,512]{1,0:T(8,128)S(1)} %copy-done.3, f32[264,512]{1,0:T(8,128)} %collective-permute-done.2.refs_3_, ...), custom_call_target="tpu_custom_call" | custom-call | flops 5368709120 | bytes 13631488 | tf_op jit(solution)/shard_map/couple_late/pallas_call | solution.py:273
  126.8 26.1 %all_to_all.21 = f32[16,40,256]{2,1,0:T(8,128)S(1)} all-to-all(f32[16,40,256]{2,1,0:T(8,128)S(1)} %bitcast.7), channel_id=1, replica_groups=mesh['row'=8,'col'=16] {'col'}, dimensions={0} | all-to-all | bytes 1310720 | tf_op jit(solution)/shard_map/all_to_all | solution.py:437
  153.8 10.8 %all-to-all-start.1 = ((f32[16,40,256]{2,1,0:T(8,128)}), f32[16,40,256]{2,1,0:T(8,128)S(1)}, u32[]{:S(2)}, u32[]{:S(2)}) async-start(f32[16,40,256]{2,1,0:T(8,128)} %broadcast_in_dim.2), calls=%async_computation.1 | async-start | bytes 1310720 | tf_op jit(solution)/shard_map/all_to_all | solution.py:437
  164.7 3.5 %collective-permute-start.18 = (f32[128,512]{1,0:T(8,128)}, f32[128,512]{1,0:T(8,128)S(1)}, u32[]{:S(2)}, u32[]{:S(2)}) collective-permute-start(f32[128,512]{1,0:T(8,128)} %get-tuple-element.12), channel_id=1, source_target_pairs={{0,64},{16,80},{32,96},{48,112},{64,0},{80,16},{96,32},{112,48},{1... | collective-permute-start | bytes 786440 | tf_op jit(solution)/shard_map/ppermute | solution.py:481
  168.2 2.5 %collective-permute-start.19 = (f32[128,512]{1,0:T(8,128)S(1)}, f32[128,512]{1,0:T(8,128)S(1)}, u32[]{:S(2)}, u32[]{:S(2)}) collective-permute-start(f32[128,512]{1,0:T(8,128)S(1)} %copy-done.32), channel_id=1, source_target_pairs={{0,96},{16,112},{32,0},{48,16},{64,32},{80,48},{96,64},{112,80},{1... | collective-permute-start | bytes 786440 | tf_op jit(solution)/shard_map/ppermute | solution.py:481
  174.6 10.9 %collective-permute-start.21 = (f32[128,512]{1,0:T(8,128)S(1)}, f32[128,512]{1,0:T(8,128)S(1)}, u32[]{:S(2)}, u32[]{:S(2)}) collective-permute-start(f32[128,512]{1,0:T(8,128)S(1)} %get-tuple-element.20), channel_id=1, source_target_pairs={{0,32},{16,48},{32,64},{48,80},{64,96},{80,112},{96,0},{112,16},{1... | collective-permute-start | bytes 786440 | tf_op jit(solution)/shard_map/ppermute | solution.py:483
  188.8 2.9 %collective-permute-done.21.refs_5_ = f32[128,512]{1,0:T(8,128)S(1)} collective-permute-done((f32[128,512]{1,0:T(8,128)S(1)}, f32[128,512]{1,0:T(8,128)S(1)}, u32[]{:S(2)}, u32[]{:S(2)}) %collective-permute-start.21) | collective-permute-done | bytes 262176 | tf_op jit(solution)/shard_map/ppermute | solution.py:483
  198.1 2.9 %forms.1 = (f32[512,512]{1,0:T(8,128)}, f32[8,128]{1,0:T(8,128)S(1)}) custom-call(f32[16,40,256]{2,1,0:T(8,128)S(1)} %all-to-all-done.1.packed, f32[512,512]{1,0:T(8,128)S(1)} %copy-done.6, f32[128,512]{1,0:T(8,128)S(1)} %copy-done.30, f32[128,512]{1,0:T(8,128)S(1)} %collective-permute-done.17.refs_1_, f32[128,512]{1,0:T(8,128)S(1)} %copy-done.21, ...), custom_call_target="tpu_custom_call" | custom-call | flops 1610612736 | bytes 5242880 | tf_op jit(solution)/shard_map/forms/pallas_call | solution.py:391
  201.0 14.7 %all_to_all.22 = f32[8,1,128]{2,1,0:T(1,128)} all-to-all(f32[8,1,128]{2,1,0:T(1,128)S(1)} %bitcast.8), channel_id=1, replica_groups=mesh['row'=8,'col'=16] {'row'}, dimensions={0} | all-to-all | bytes 8192 | tf_op jit(solution)/shard_map/all_to_all | solution.py:437
  (106 shorter events, 35.5 us)
Async XLA Ops:
  0.6 11.5 %collective-permute-start.10 = (f32[512,512]{1,0:T(8,128)}, f32[512,512]{1,0:T(8,128)S(1)}, u32[]{:S(2)}, u32[]{:S(2)}) collective-permute-start(f32[512,512]{1,0:T(8,128)} %refs_10_.1), channel_id=1, source_target_pairs={{0,1},{1,0},{2,3},{3,2},{4,5},{5,4},{6,7},{7,6},{8,9},{9,8},{10,11... | collective-permute-start | bytes 3145736 | tf_op jit(solution)/shard_map/ppermute | solution.py:464
  0.7 25.4 %collective-permute-start.7 = (f32[512,512]{1,0:T(8,128)}, f32[512,512]{1,0:T(8,128)}, u32[]{:S(2)}, u32[]{:S(2)}) collective-permute-start(f32[512,512]{1,0:T(8,128)} %refs_10_.1), channel_id=1, source_target_pairs={{0,8},{1,9},{2,10},{3,11},{4,12},{5,13},{6,14},{7,15},{8,1},{9,0},... | collective-permute-start | bytes 3145736 | tf_op jit(solution)/shard_map/ppermute | solution.py:458
  5.2 28.1 %collective-permute-start = (f32[520,512]{1,0:T(8,128)}, f32[520,512]{1,0:T(8,128)S(1)}, u32[]{:S(2)}, u32[]{:S(2)}) collective-permute-start(f32[520,512]{1,0:T(8,128)} %pick.1.refs_0_), channel_id=1, source_target_pairs={{0,32},{16,48},{32,64},{48,80},{64,96},{80,112},{96,0},{112,16},{1... | collective-permute-start | bytes 3194888 | tf_op jit(solution)/shard_map/ppermute | solution.py:462
  7.2 26.9 %collective-permute-start.1 = (f32[520,512]{1,0:T(8,128)}, f32[520,512]{1,0:T(8,128)S(1)}, u32[]{:S(2)}, u32[]{:S(2)}) collective-permute-start(f32[520,512]{1,0:T(8,128)} %pick.1.refs_0_), channel_id=1, source_target_pairs={{0,96},{16,112},{32,0},{48,16},{64,32},{80,48},{96,64},{112,80},{1... | collective-permute-start | bytes 3194888 | tf_op jit(solution)/shard_map/ppermute | solution.py:463
  9.4 44.2 %collective-permute-start.4 = (f32[520,512]{1,0:T(8,128)}, f32[520,512]{1,0:T(8,128)}, u32[]{:S(2)}, u32[]{:S(2)}) collective-permute-start(f32[520,512]{1,0:T(8,128)} %pick.1.refs_0_), channel_id=1, source_target_pairs={{0,16},{16,0},{32,48},{48,32},{64,80},{80,64},{96,112},{112,96},{1... | collective-permute-start | bytes 3194888 | tf_op jit(solution)/shard_map/ppermute | solution.py:465
  12.1 26.7 %collective-permute-start.6 = (f32[512,512]{1,0:T(8,128)S(1)}, f32[512,512]{1,0:T(8,128)S(1)}, u32[]{:S(2)}, u32[]{:S(2)}) collective-permute-start(f32[512,512]{1,0:T(8,128)S(1)} %copy-done.4), channel_id=1, source_target_pairs={{0,7},{1,6},{2,1},{3,0},{4,3},{5,2},{6,5},{7,4},{8,15},{9,14},{10,... | collective-permute-start | bytes 3145736 | tf_op jit(solution)/shard_map/ppermute | solution.py:460
  26.2 26.1 %collective-permute-start.5 = (f32[512,512]{1,0:T(8,128)S(1)}, f32[512,512]{1,0:T(8,128)}, u32[]{:S(2)}, u32[]{:S(2)}) collective-permute-start(f32[512,512]{1,0:T(8,128)S(1)} %copy-done.4), channel_id=1, source_target_pairs={{0,2},{1,3},{2,4},{3,5},{4,6},{5,7},{6,0},{7,1},{8,10},{9,11},{10,... | collective-permute-start | bytes 3145736 | tf_op jit(solution)/shard_map/ppermute | solution.py:459
  33.3 27.6 %collective-permute-start.9 = (f32[512,512]{1,0:T(8,128)}, f32[512,512]{1,0:T(8,128)}, u32[]{:S(2)}, u32[]{:S(2)}) collective-permute-start(f32[512,512]{1,0:T(8,128)} %collective-permute-done.7.refs_9_.refs_14_), channel_id=1, source_target_pairs={{0,6},{1,7},{2,0},{3,1},{4,2},{5,3},{6,4},{7,5},{8,14},{9,15},{10,... | collective-permute-start | bytes 3145736 | tf_op jit(solution)/shard_map/ppermute | solution.py:467
  34.1 23.6 %collective-permute-start.2 = (f32[264,512]{1,0:T(8,128)S(1)}, f32[264,512]{1,0:T(8,128)}, u32[]{:S(2)}, u32[]{:S(2)}) collective-permute-start(f32[264,512]{1,0:T(8,128)S(1)} %slice.20), channel_id=1, source_target_pairs={{0,32},{16,48},{32,64},{48,80},{64,96},{80,112},{96,0},{112,16},{1... | collective-permute-start | bytes 1622024 | tf_op jit(solution)/shard_map/ppermute | solution.py:469
  39.8 13.8 %collective-permute-start.3 = (f32[256,512]{1,0:T(8,128)S(1)}, f32[256,512]{1,0:T(8,128)S(1)}, u32[]{:S(2)}, u32[]{:S(2)}) collective-permute-start(f32[256,512]{1,0:T(8,128)S(1)} %slice.21), channel_id=1, source_target_pairs={{0,96},{16,112},{32,0},{48,16},{64,32},{80,48},{96,64},{112,80},{1... | collective-permute-start | bytes 1572872 | tf_op jit(solution)/shard_map/ppermute | solution.py:469
  52.2 26.2 %collective-permute-start.8 = (f32[512,512]{1,0:T(8,128)}, f32[512,512]{1,0:T(8,128)S(1)}, u32[]{:S(2)}, u32[]{:S(2)}) collective-permute-start(f32[512,512]{1,0:T(8,128)} %collective-permute-done.7.refs_9_.refs_14_), channel_id=1, source_target_pairs={{0,2},{1,3},{2,4},{3,5},{4,6},{5,7},{6,0},{7,1},{8,10},{9,11},{10,... | collective-permute-start | bytes 3145736 | tf_op jit(solution)/shard_map/ppermute | solution.py:466
  53.6 46.6 %collective-permute-start.15 = (f32[512,512]{1,0:T(8,128)}, f32[512,512]{1,0:T(8,128)S(1)}, u32[]{:S(2)}, u32[]{:S(2)}) collective-permute-start(f32[512,512]{1,0:T(8,128)} %collective-permute-done.5.refs_7_.refs_11_), channel_id=1, source_target_pairs={{0,3},{1,2},{2,4},{3,5},{4,6},{5,7},{6,1},{7,0},{8,11},{9,10},{10,... | collective-permute-start | bytes 3145736 | tf_op jit(solution)/shard_map/ppermute | solution.py:470
  53.6 70.3 %collective-permute-start.12 = (f32[520,512]{1,0:T(8,128)}, f32[520,512]{1,0:T(8,128)}, u32[]{:S(2)}, u32[]{:S(2)}) collective-permute-start(f32[520,512]{1,0:T(8,128)} %collective-permute-done.4.refs_5_), channel_id=1, source_target_pairs={{0,96},{16,112},{32,0},{48,16},{64,32},{80,48},{96,64},{112,80},{1... | collective-permute-start | bytes 3194888 | tf_op jit(solution)/shard_map/ppermute | solution.py:472
  57.7 66.2 %collective-permute-start.11 = (f32[520,512]{1,0:T(8,128)}, f32[520,512]{1,0:T(8,128)}, u32[]{:S(2)}, u32[]{:S(2)}) collective-permute-start(f32[520,512]{1,0:T(8,128)} %collective-permute-done.4.refs_5_), channel_id=1, source_target_pairs={{0,32},{16,48},{32,64},{48,80},{64,96},{80,112},{96,0},{112,16},{1... | collective-permute-start | bytes 3194888 | tf_op jit(solution)/shard_map/ppermute | solution.py:471
  61.0 63.0 %collective-permute-start.16 = (f32[512,512]{1,0:T(8,128)}, f32[512,512]{1,0:T(8,128)}, u32[]{:S(2)}, u32[]{:S(2)}) collective-permute-start(f32[512,512]{1,0:T(8,128)} %collective-permute-done.9.refs_11_.refs_16_), channel_id=1, source_target_pairs={{0,6},{1,7},{2,0},{3,1},{4,2},{5,3},{6,4},{7,5},{8,14},{9,15},{10,... | collective-permute-start | bytes 3145736 | tf_op jit(solution)/shard_map/ppermute | solution.py:473
  79.5 44.4 %collective-permute-start.13 = (f32[264,512]{1,0:T(8,128)}, f32[264,512]{1,0:T(8,128)}, u32[]{:S(2)}, u32[]{:S(2)}) collective-permute-start(f32[264,512]{1,0:T(8,128)} %collective-permute-done.2.refs_3_), channel_id=1, source_target_pairs={{0,16},{16,0},{32,48},{48,32},{64,80},{80,64},{96,112},{112,96},{1... | collective-permute-start | bytes 1622024 | tf_op jit(solution)/shard_map/ppermute | solution.py:474
  101.1 19.1 %collective-permute-start.14 = (f32[256,512]{1,0:T(8,128)}, f32[256,512]{1,0:T(8,128)}, u32[]{:S(2)}, u32[]{:S(2)}) collective-permute-start(f32[256,512]{1,0:T(8,128)} %copy-done.17), channel_id=1, source_target_pairs={{0,16},{16,0},{32,48},{48,32},{64,80},{80,64},{96,112},{112,96},{1... | collective-permute-start | bytes 1572872 | tf_op jit(solution)/shard_map/ppermute | solution.py:474
  120.2 50.5 %collective-permute-start.20 = (f32[512,512]{1,0:T(8,128)}, f32[512,512]{1,0:T(8,128)S(1)}, u32[]{:S(2)}, u32[]{:S(2)}) collective-permute-start(f32[512,512]{1,0:T(8,128)} %get-tuple-element.14), channel_id=1, source_target_pairs={{0,16},{16,0},{32,48},{48,32},{64,80},{80,64},{96,112},{112,96},{1... | collective-permute-start | bytes 3145736 | tf_op jit(solution)/shard_map/ppermute | solution.py:480
  153.8 38.7 %all-to-all-start.1 = ((f32[16,40,256]{2,1,0:T(8,128)}), f32[16,40,256]{2,1,0:T(8,128)S(1)}, u32[]{:S(2)}, u32[]{:S(2)}) async-start(f32[16,40,256]{2,1,0:T(8,128)} %broadcast_in_dim.2), calls=%async_computation.1 | async-start | bytes 1310720 | tf_op jit(solution)/shard_map/all_to_all | solution.py:437
  164.7 20.7 %collective-permute-start.18 = (f32[128,512]{1,0:T(8,128)}, f32[128,512]{1,0:T(8,128)S(1)}, u32[]{:S(2)}, u32[]{:S(2)}) collective-permute-start(f32[128,512]{1,0:T(8,128)} %get-tuple-element.12), channel_id=1, source_target_pairs={{0,64},{16,80},{32,96},{48,112},{64,0},{80,16},{96,32},{112,48},{1... | collective-permute-start | bytes 786440 | tf_op jit(solution)/shard_map/ppermute | solution.py:481
  168.2 18.0 %collective-permute-start.19 = (f32[128,512]{1,0:T(8,128)S(1)}, f32[128,512]{1,0:T(8,128)S(1)}, u32[]{:S(2)}, u32[]{:S(2)}) collective-permute-start(f32[128,512]{1,0:T(8,128)S(1)} %copy-done.32), channel_id=1, source_target_pairs={{0,96},{16,112},{32,0},{48,16},{64,32},{80,48},{96,64},{112,80},{1... | collective-permute-start | bytes 786440 | tf_op jit(solution)/shard_map/ppermute | solution.py:481
  170.8 16.7 %collective-permute-start.23 = (f32[128,512]{1,0:T(8,128)S(1)}, f32[128,512]{1,0:T(8,128)S(1)}, u32[]{:S(2)}, u32[]{:S(2)}) collective-permute-start(f32[128,512]{1,0:T(8,128)S(1)} %get-tuple-element.18), channel_id=1, source_target_pairs={{0,96},{16,112},{32,0},{48,16},{64,32},{80,48},{96,64},{112,80},{1... | collective-permute-start | bytes 786440 | tf_op jit(solution)/shard_map/ppermute | solution.py:483
  170.8 17.3 %collective-permute-start.22 = (f32[128,512]{1,0:T(8,128)S(1)}, f32[128,512]{1,0:T(8,128)S(1)}, u32[]{:S(2)}, u32[]{:S(2)}) collective-permute-start(f32[128,512]{1,0:T(8,128)S(1)} %get-tuple-element.19), channel_id=1, source_target_pairs={{0,64},{16,80},{32,96},{48,112},{64,0},{80,16},{96,32},{112,48},{1... | collective-permute-start | bytes 786440 | tf_op jit(solution)/shard_map/ppermute | solution.py:483
  174.6 17.2 %collective-permute-start.21 = (f32[128,512]{1,0:T(8,128)S(1)}, f32[128,512]{1,0:T(8,128)S(1)}, u32[]{:S(2)}, u32[]{:S(2)}) collective-permute-start(f32[128,512]{1,0:T(8,128)S(1)} %get-tuple-element.20), channel_id=1, source_target_pairs={{0,32},{16,48},{32,64},{48,80},{64,96},{80,112},{96,0},{112,16},{1... | collective-permute-start | bytes 786440 | tf_op jit(solution)/shard_map/ppermute | solution.py:483
  (34 other events, 246.7 us)
